TPU v7x, 256 devices: a whole 4x4x8 slice. The times are simulated.
256 devices in a mesh: section: 16 (over z_lo, y), ctx: 4 (over x), tensor: 4 (over z_hi, core).
Axes of the slice: x: 4, y: 4, z: 8 (z_hi: 2, z_lo: 4; z = z_hi * 4 + z_lo), core: 2. Of those that a mesh axis runs over, the one named last changes fastest.
Arguments:
- arriving: bfloat16 [16, 1024, 4096], P('section', 'ctx', 'tensor')
- stored: bfloat16 [16, 1024, 4096], P('section', 'ctx', 'tensor')
- docs_forward: int32 [16, 1024], P('section', 'ctx'), may hold values from 0 to 3, never falling along the last dimension, each value on 1 to 512 neighbouring positions
- docs_backward: int32 [16, 1024], P('section', 'ctx'), may hold values from 0 to 3, never falling along the last dimension, each value on 1 to 512 neighbouring positions
- norm_gain: bfloat16 [16, 4096], P('section')
- query_weight: bfloat16 [16, 4096, 4096], P('section', 'ctx', 'tensor')
- key_weight: bfloat16 [16, 4096, 512], P('section', 'ctx', 'tensor')
- value_projection_weight: bfloat16 [16, 4096, 512], P('section', 'ctx', 'tensor'), may hold values from -0.09375 to 0.09375
- out_weight: bfloat16 [16, 4096, 4096], P('section', 'tensor', 'ctx'), may hold values from -0.375 to 0.375
Outputs:
- forward_output: bfloat16 [16, 1024, 4096], P('section', 'ctx', 'tensor')
- stashed: bfloat16 [16, 1024, 4096], P('section', 'ctx', 'tensor')
- rebuilt: bfloat16 [16, 1024, 4096], P('section', 'ctx', 'tensor')
Inputs may be any that keep to these rules, and one draw needn't show every extreme that they name: `docs_forward`: each row holds 4 packed documents: ids never fall, each document has 1 to 512 tokens, one exactly 512. `docs_backward`: each row holds 4 packed documents: ids never fall, each document has 1 to 512 tokens, one exactly 512.
All inputs are finite; a program needn't handle non-finite values.
Results may differ from a plain program's by a relative error of at most 0.0066.
Values may be sent and summed in bfloat16 or wider, within the bound.
No kernel may reach another device: no remote copies, remote signals or barrier semaphores. Data moves between devices by JAX's collectives and lax.ppermute only.
A program may use at most 128 MiB of HBM per device.

v0:
```python
import math
import jax
import jax.numpy as jnp
from jax import lax
from jax.sharding import PartitionSpec as P

HEAD = 128
QH = 32
KVH = 4
norm_epsilon = 1e-05
rope_base = 500000.0


def from_partner(block, axis, distance):
    count = lax.axis_size(axis)
    route = []
    for low in range(count):
        high = low | 1 << distance
        if high != low and high < count:
            route += [(low, high), (high, low)]
    return lax.ppermute(block, axis, route)


def normalize(inputs, gain_row):
    values = inputs.astype(jnp.float32)
    mean_square = jnp.mean(values * values, axis=-1, keepdims=True)
    return (values * lax.rsqrt(mean_square + norm_epsilon) * gain_row.astype(jnp.float32)).astype(
        jnp.bfloat16
    )


def rotary(values, positions, head_size):
    half_size = head_size // 2
    tokens = values.shape[0]
    shaped = values.reshape(tokens, -1, head_size)
    exponent = jnp.arange(half_size).astype(jnp.float32) * (2.0 / head_size)
    inverse = jnp.exp(-exponent * math.log(rope_base))
    angles = positions.astype(jnp.float32)[:, None] * inverse[None, :]
    cosine_lookup = jnp.cos(angles)[:, None, :]
    sine_table = jnp.sin(angles)[:, None, :]
    first_half = shaped[:, :, :half_size]
    second_half = shaped[:, :, half_size:]
    turned = jnp.concatenate(
        (
            first_half * cosine_lookup - second_half * sine_table,
            second_half * cosine_lookup + first_half * sine_table,
        ),
        axis=2,
    )
    return turned.reshape(tokens, -1)


def attend(queries, key_rows, value_rows, query_positions, key_positions, query_docs, key_docs):
    query_count = queries.shape[0]
    key_count = key_rows.shape[0]
    group_count = key_rows.shape[1] // HEAD
    group_size = QH // KVH
    grouped = queries.reshape(query_count, group_count, group_size, HEAD)
    key_heads = key_rows.reshape(key_count, group_count, HEAD)
    value_heads = value_rows.reshape(key_count, group_count, HEAD)
    permitted_mask = (key_positions[None, :] <= query_positions[:, None]) & (
        key_docs[None, :] == query_docs[:, None]
    )
    scores = jnp.einsum(
        "qkgh,skh->kgqs", grouped, key_heads, preferred_element_type=jnp.float32
    ) * (1.0 / math.sqrt(HEAD))
    masked = jnp.where(permitted_mask[None, None], scores, -jnp.inf)
    row_peak = jnp.max(masked, axis=3, keepdims=True)
    weights = jnp.exp(masked - row_peak)
    totals = jnp.sum(weights, axis=3, keepdims=True)
    probabilities = weights.astype(jnp.bfloat16)
    mixed_heads = jnp.einsum(
        "kgqs,skh->qkgh", probabilities, value_heads, preferred_element_type=jnp.float32
    )
    mixed_heads = mixed_heads / jnp.transpose(totals, (2, 0, 1, 3))
    return mixed_heads.reshape(query_count, -1).astype(jnp.bfloat16)


def body(
    arriving,
    stored,
    docs_forward,
    docs_backward,
    norm_gain,
    query_weight,
    key_weight,
    value_projection_weight,
    out_weight,
):
    tok_rows = arriving.shape[1]
    top_bit = lax.axis_size("section").bit_length() - 2
    stashed, fetched = from_partner((arriving, stored), "section", top_bit)
    inputs = jnp.concatenate((arriving[0], fetched[0]), axis=0)
    full_rows = lax.all_gather(inputs, "tensor", axis=1, tiled=True)
    normed = normalize(full_rows, norm_gain[0])
    key_width = key_weight.shape[2]
    query_full, key_full, value_full, out_full = (
        lax.all_gather(query_weight[0], "ctx", axis=0, tiled=True),
        lax.all_gather(key_weight[0], "ctx", axis=0, tiled=True),
        lax.all_gather(value_projection_weight[0], "ctx", axis=0, tiled=True),
        lax.all_gather(out_weight[0], "ctx", axis=1, tiled=True),
    )
    query_raw = jnp.dot(normed, query_full, preferred_element_type=jnp.float32)
    key_raw = jnp.dot(normed, key_full, preferred_element_type=jnp.float32)
    value_raw = jnp.dot(normed, value_full, preferred_element_type=jnp.float32)
    offset = lax.axis_index("ctx") * tok_rows
    local_pos = offset + jnp.arange(tok_rows, dtype=jnp.int32)
    both_pos = jnp.concatenate((local_pos, local_pos), axis=0)
    queries = rotary(query_raw, both_pos, HEAD).astype(jnp.bfloat16)
    key_rows = rotary(key_raw, both_pos, HEAD).astype(jnp.bfloat16)
    value_rows = value_raw.astype(jnp.bfloat16)
    docs_pair = jnp.stack((docs_forward[0], docs_backward[0]), axis=0)
    all_keys, all_values, all_docs = (
        lax.all_gather(key_rows.reshape(2, tok_rows, key_width), "ctx", axis=1, tiled=True),
        lax.all_gather(value_rows.reshape(2, tok_rows, key_width), "ctx", axis=1, tiled=True),
        lax.all_gather(docs_pair, "ctx", axis=1, tiled=True),
    )
    key_pos = jnp.arange(all_keys.shape[1], dtype=jnp.int32)
    mixed_parts = []
    for batch_index in range(2):
        mixed_parts.append(
            attend(
                queries[batch_index * tok_rows : (batch_index + 1) * tok_rows],
                all_keys[batch_index],
                all_values[batch_index],
                local_pos,
                key_pos,
                docs_pair[batch_index],
                all_docs[batch_index],
            )
        )
    mixed_heads = jnp.concatenate(mixed_parts, axis=0)
    head_terms = jnp.dot(mixed_heads, out_full, preferred_element_type=jnp.float32)
    head_total = lax.psum_scatter(head_terms, "tensor", scatter_dimension=1, tiled=True)
    result = (inputs.astype(jnp.float32) + head_total).astype(jnp.bfloat16)
    return (result[:tok_rows][None], stashed, result[tok_rows:][None])


def solution(mesh):
    return jax.shard_map(
        body,
        mesh=mesh,
        in_specs=(
            P("section", "ctx", "tensor"),
            P("section", "ctx", "tensor"),
            P("section", "ctx"),
            P("section", "ctx"),
            P("section", None),
            P("section", "ctx", "tensor"),
            P("section", "ctx", "tensor"),
            P("section", "ctx", "tensor"),
            P("section", "tensor", "ctx"),
        ),
        out_specs=(
            P("section", "ctx", "tensor"),
            P("section", "ctx", "tensor"),
            P("section", "ctx", "tensor"),
        ),
        check_vma=False,
    )
```

profile of v0, /device:TPU:1, one launch (start us, length us, event | category | flops | bytes accessed | tf_op | source)
XLA Modules:
  0.0 493.1 jit_solution(5165739500692440030)
XLA Ops:
  7.2 0.0 all-gather.10.cloned.1.call-start
  7.2 3.9 collective-permute-start
  11.1 22.4 %collective-permute-done = bf16[1,256,1024]{2,1,0:T(8,128)(2,1)S(1)} collective-permute-done((bf16[1,256,1024]{2,1,0:T(8,128)(2,1)}, bf16[1,256,1024]{2,1,0:T(8,128)(2,1)S(1)}, u32[]{:S(2)}, u32[]{:S(2)}) %collective-permute-start) | collective-permute-done | bytes 524320 | tf_op jit(solution)/shard_map/ppermute | solution.py:21
  33.6 2.1 pad_maximum_fusion
  35.7 0.0 all-gather.14.cloned.1.call-start
  35.7 0.7 all-gather.14.cloned.1.call-update
  36.4 0.0 all-gather.12.cloned.1.call-start
  36.5 0.7 all-gather.12.cloned.1.call-update
  37.1 0.0 all-gather.16.cloned.1.call-start
  37.2 0.5 all-gather.16.cloned.1.call-update
  37.7 0.0 all-gather.18.cloned.1.call-start
  37.8 0.5 all-gather.18.cloned.1.call-update
  38.3 0.0 reduce-scatter.2.cloned.1.call-start
  38.4 0.7 mul.176
  39.1 0.7 pad_add_fusion
  39.8 9.1 %all_gather.27 = s32[2,1024]{1,0:T(2,128)S(1)} all-gather(s32[2,256]{1,0:T(2,128)S(1)} %pad_add_fusion), channel_id=1, replica_groups=mesh['section'=16,'ctx'=4,'tensor'=4] {'ctx'}, dimensions={1}, use_global_device_ids=true | all-gather | bytes 10240 | tf_op jit(solution)/shard_map/all_gather | solution.py:116
  49.0 1.0 multiply_cosine_fusion
  50.0 0.7 fusion.36
  50.7 55.7 %all-gather.10.cloned.1.call-done = bf16[512,4096]{1,0:T(8,128)(2,1)} async-done(((bf16[512,1024]{1,0:T(8,128)(2,1)}), bf16[512,4096]{1,0:T(8,128)(2,1)}) %all-gather.10.cloned.1.call-update) | async-done | bytes 4194320 | tf_op jit(solution)/shard_map/all_gather | solution.py:94
  106.3 3.1 fusion
  109.4 20.0 %all-gather.14.cloned.1.call-done = bf16[1,4096,128]{2,1,0:T(8,128)(2,1)} async-done(((bf16[1,1024,128]{2,1,0:T(8,128)(2,1)}), bf16[1,4096,128]{2,1,0:T(8,128)(2,1)}) %all-gather.14.cloned.1.call-update) | async-done | bytes 1048592 | tf_op jit(solution)/shard_map/all_gather | solution.py:99
  129.5 4.1 convolution_bitcast_fusion
  133.6 0.6 fusion.51
  134.2 0.1 copy.20
  134.3 23.9 %all-gather.12.cloned.1.call-done = bf16[1,4096,128]{2,1,0:T(8,128)(2,1)} async-done(((bf16[1,1024,128]{2,1,0:T(8,128)(2,1)}), bf16[1,4096,128]{2,1,0:T(8,128)(2,1)}) %all-gather.12.cloned.1.call-update) | async-done | bytes 1048592 | tf_op jit(solution)/shard_map/all_gather | solution.py:100
  158.2 3.8 convolution_convert_fusion
  162.0 0.1 copy.12
  162.1 11.3 %all_gather.29 = bf16[2,1024,128]{2,1,0:T(8,128)(2,1)S(1)} all-gather(bf16[2,256,128]{2,1,0:T(8,128)(2,1)S(1)} %bitcast.131), channel_id=1, replica_groups=mesh['section'=16,'ctx'=4,'tensor'=4] {'ctx'}, dimensions={1}, use_global_device_ids=true | all-gather | bytes 655360 | tf_op jit(solution)/shard_map/all_gather | solution.py:114
  173.4 12.5 %all_gather.26 = bf16[2,1024,128]{1,2,0:T(8,128)(2,1)S(1)} all-gather(bf16[2,256,128]{1,2,0:T(8,128)(2,1)S(1)} %copy.12), channel_id=1, replica_groups=mesh['section'=16,'ctx'=4,'tensor'=4] {'ctx'}, dimensions={1}, use_global_device_ids=true | all-gather | bytes 655360 | tf_op jit(solution)/shard_map/all_gather | solution.py:115
  186.0 64.5 %all-gather.16.cloned.1.call-done = bf16[1,4096,1024]{2,1,0:T(8,128)(2,1)} async-done(((bf16[1,1024,1024]{2,1,0:T(8,128)(2,1)}), bf16[1,4096,1024]{2,1,0:T(8,128)(2,1)}) %all-gather.16.cloned.1.call-update) | async-done | bytes 8388624 | tf_op jit(solution)/shard_map/all_gather | solution.py:98
  250.5 8.2 %fusion.21 = f32[64,8,8,128]{3,1,2,0:T(8,128)S(1)} fusion(bf16[1,4096,1024]{2,1,0:T(8,128)(2,1)} %all-gather.16.cloned.1.call-done, bf16[512,4096]{1,0:T(8,128)(2,1)} %all-gather.10.cloned.1.call-done, f32[4096]{0:T(1024)S(1)} %bitcast.137, f32[512]{0:T(512)S(1)} %add_rsqrt_fusion), kind=kOutput, calls=%fused_computation.28 | convolution fusion | flops 4303355904 | bytes 14698496 | tf_op jit(solution)/shard_map/dot_general | solution.py:103
  258.7 0.5 copy.23
  259.2 0.7 fusion.64
  259.9 0.8 subtract_convert_fusion
  260.7 1.6 fusion.11
  262.3 1.7 fusion.12
  264.0 3.7 fusion.7
  267.7 2.3 divide_convert_fusion.1
  270.0 2.2 divide_convert_fusion
  272.2 66.4 %all-gather.18.cloned.1.call-done = bf16[1,1024,4096]{2,1,0:T(8,128)(2,1)} async-done(((bf16[1,1024,1024]{2,1,0:T(8,128)(2,1)}), bf16[1,1024,4096]{2,1,0:T(8,128)(2,1)}) %all-gather.18.cloned.1.call-update) | async-done | bytes 8388624 | tf_op jit(solution)/shard_map/all_gather | solution.py:101
  338.6 10.2 %fusion.3 = f32[512,4096]{1,0:T(8,128)} fusion(bf16[1,1024,4096]{2,1,0:T(8,128)(2,1)} %all-gather.18.cloned.1.call-done, bf16[256,1024]{0,1:T(8,128)(2,1)S(1)} %bitcast.130, bf16[256,1024]{0,1:T(8,128)(2,1)S(1)} %bitcast.129), kind=kOutput, calls=%fused_computation.7 | convolution fusion | flops 4297064448 | bytes 17825792 | tf_op jit(solution)/shard_map/dot_general | solution.py:133
  348.9 1.0 copy-done
  349.9 2.3 collective-permute-start.1
  352.2 22.7 %collective-permute-done.1 = bf16[1,256,1024]{2,1,0:T(8,128)(2,1)S(1)} collective-permute-done((bf16[1,256,1024]{2,1,0:T(8,128)(2,1)S(1)}, bf16[1,256,1024]{2,1,0:T(8,128)(2,1)S(1)}, u32[]{:S(2)}, u32[]{:S(2)}) %collective-permute-start.1) | collective-permute-done | bytes 524320 | tf_op jit(solution)/shard_map/ppermute | solution.py:21
  374.9 107.6 %reduce-scatter.2.cloned.1.call-done = f32[512,1024]{1,0:T(8,128)} async-done(((f32[512,4096]{1,0:T(8,128)}), f32[512,1024]{1,0:T(8,128)}) %reduce-scatter.2.cloned.1.call-update) | async-done | bytes 2097168 | tf_op jit(solution)/shard_map/reduce_scatter | solution.py:134
  482.5 1.9 add_convert_fusion
  484.4 1.0 slice_bitcast_fusion
  485.5 0.8 copy.29
  (13 shorter events, 0.1 us)
Async XLA Ops:
  7.2 42.8 %copy-start.1 = (s32[1,256]{1,0:T(1,128)S(1)}, s32[1,256]{1,0:T(1,128)}, u32[]{:S(2)}) copy-start(s32[1,256]{1,0:T(1,128)} %param.11) | copy-start | bytes 3076
  7.2 42.8 %copy-start.2 = (s32[1,256]{1,0:T(1,128)S(1)}, s32[1,256]{1,0:T(1,128)}, u32[]{:S(2)}) copy-start(s32[1,256]{1,0:T(1,128)} %param.12) | copy-start | bytes 3076
  7.2 99.2 %all-gather.10.cloned.1.call-start = ((), (), s32[]{:S(2)}) async-start(), calls=%async_computation.1 | async-start | bytes 5242880 | tf_op jit(solution)/shard_map/all_gather | solution.py:94
  7.2 26.3 %collective-permute-start = (bf16[1,256,1024]{2,1,0:T(8,128)(2,1)}, bf16[1,256,1024]{2,1,0:T(8,128)(2,1)S(1)}, u32[]{:S(2)}, u32[]{:S(2)}) collective-permute-start(bf16[1,256,1024]{2,1,0:T(8,128)(2,1)} %param.10), channel_id=1, source_target_pairs={{0,128},{128,0},{16,144},{144,16},{32,160},{160,32},{48,176},{176,... | collective-permute-start | bytes 1572872 | tf_op jit(solution)/shard_map/ppermute | solution.py:21
  35.7 93.8 %all-gather.14.cloned.1.call-start = ((), (), s32[]{:S(2)}) async-start(), calls=%async_computation.4 | async-start | bytes 1310720 | tf_op jit(solution)/shard_map/all_gather | solution.py:99
  36.4 121.8 %all-gather.12.cloned.1.call-start = ((), (), s32[]{:S(2)}) async-start(), calls=%async_computation.3 | async-start | bytes 1310720 | tf_op jit(solution)/shard_map/all_gather | solution.py:100
  37.1 213.4 %all-gather.16.cloned.1.call-start = ((), (), s32[]{:S(2)}) async-start(), calls=%async_computation.5 | async-start | bytes 10485760 | tf_op jit(solution)/shard_map/all_gather | solution.py:98
  37.7 300.9 %all-gather.18.cloned.1.call-start = ((), (), s32[]{:S(2)}) async-start(), calls=%async_computation.6 | async-start | bytes 10485760 | tf_op jit(solution)/shard_map/all_gather | solution.py:101
  38.3 444.2 %reduce-scatter.2.cloned.1.call-start = ((), (), s32[]{:S(2)}) async-start(), calls=%async_computation.2 | async-start | bytes 10485760 | tf_op jit(solution)/shard_map/reduce_scatter | solution.py:134
  348.8 1.0 copy-start
  349.9 25.0 %collective-permute-start.1 = (bf16[1,256,1024]{2,1,0:T(8,128)(2,1)S(1)}, bf16[1,256,1024]{2,1,0:T(8,128)(2,1)S(1)}, u32[]{:S(2)}, u32[]{:S(2)}) collective-permute-start(bf16[1,256,1024]{2,1,0:T(8,128)(2,1)S(1)} %copy-done), channel_id=1, source_target_pairs={{0,128},{128,0},{16,144},{144,16},{32,160},{160,32},{48,176},{176,... | collective-permute-start | bytes 1572872 | tf_op jit(solution)/shard_map/ppermute | solution.py:21
Sparse Core Ops, SparseCore 0:
  35.8 70.5 all-gather.9
  108.1 21.2 all-gather.13
  131.3 26.8 all-gather.11
  159.8 90.6 all-gather.15
  252.2 86.4 all-gather.17
  349.0 133.4 reduce-scatter.1
where the time goes:
time: 493 us
  waiting for transfers between devices  386 us (78%)
  matrix products  34.1 us (7%)
  blocking collectives  33 us (7%)
  other arithmetic  15.3 us (3%)
  between operations  14.3 us (3%)
  starting transfers between devices  6.4 us (1%)
    reduce_scatter x1, waiting for transfers between devices, body(): lax.psum_scatter(head_terms, 'tensor', scatter_dimension=1, tiled=True)  108 us
    all_gather x1, waiting for transfers between devices, body(): lax.all_gather(out_weight[0], 'ctx', axis=1, tiled=True)  66.4 us
    all_gather x1, waiting for transfers between devices, body(): lax.all_gather(query_weight[0], 'ctx', axis=0, tiled=True)  64.5 us
    all_gather x1, waiting for transfers between devices, body(): full_rows = lax.all_gather(inputs, 'tensor', axis=1, tiled=True)  55.7 us
    ppermute x2, waiting for transfers between devices, from_partner(): return lax.ppermute(block, axis, route)  45.1 us
    all_gather x1, waiting for transfers between devices, body(): lax.all_gather(value_projection_weight[0], 'ctx', axis=0, tiled=True)  23.9 us
    all_gather x1, waiting for transfers between devices, body(): lax.all_gather(key_weight[0], 'ctx', axis=0, tiled=True)  20 us
    all_gather x1, blocking collectives, body(): lax.all_gather(value_rows.reshape(2, tok_rows, key_width), 'ctx', axis=1,...  12.5 us
  transfers between devices with their start and end apart: 8, of which 8 were waited for; matrix products, arithmetic and copies ran while one was open for 7% of the time, Pallas kernels for 0%

commit v1 on v0

--- a/solution.py
+++ b/solution.py
@@ -96,7 +96,9 @@
     key_width = key_weight.shape[2]
     query_full, key_full, value_full, out_full = (
         lax.all_gather(query_weight[0], "ctx", axis=0, tiled=True),
-        lax.all_gather(key_weight[0], "ctx", axis=0, tiled=True),
+        jnp.concatenate(
+            lax.all_to_all(jnp.stack([key_weight[0]] * lax.axis_size("ctx")), "ctx", 0, 0), axis=0
+        ),
         lax.all_gather(value_projection_weight[0], "ctx", axis=0, tiled=True),
         lax.all_gather(out_weight[0], "ctx", axis=1, tiled=True),
     )

time: 493 us -> 465 us (0.943)
  waiting for transfers between devices: 386 us -> 344 us
  blocking collectives: 33 us -> 40.6 us
    all_gather x1 -> x0, waiting for transfers between devices: 20 us -> none  [body(): lax.all_gather(key_weight[0], 'ctx', axis=0, tiled=True)]
    all_gather x1, waiting for transfers between devices: 55.7 us -> 43.4 us  [body(): full_rows = lax.all_gather(inputs, 'tensor', axis=1, tiled=True)]
    all_gather x1, waiting for transfers between devices: 23.9 us -> 15.5 us  [body(): lax.all_gather(value_projection_weight[0], 'ctx', axis=0, tiled=True)]
    all_gather x1, blocking collectives: 9.1 us -> 16.7 us  [body(): lax.all_gather(docs_pair, 'ctx', axis=1, tiled=True)]
  transfers between devices with their start and end apart: 8 -> 8, of which waited for: 8 -> 7; matrix products, arithmetic and copies ran while one was open for 7% -> 8% of each run, Pallas kernels for 0% -> 0%
where the time goes in v1:
time: 465 us; the launch traced here: 464 us
  waiting for transfers between devices  344 us (74%)
  blocking collectives  40.6 us (9%)
  matrix products  33.8 us (7%)
  other arithmetic  14 us (3%)
  between operations  14 us (3%)
  starting transfers between devices  11 us (2%)
  local copies, waits for them, and re-layouts  6.32 us (1%)
    reduce_scatter x1, waiting for transfers between devices, body(): lax.psum_scatter(head_terms, 'tensor', scatter_dimension=1, tiled=True)  108 us
    all_gather x1, waiting for transfers between devices, body(): lax.all_gather(out_weight[0], 'ctx', axis=1, tiled=True)  66.3 us
    all_gather x1, waiting for transfers between devices, body(): lax.all_gather(query_weight[0], 'ctx', axis=0, tiled=True)  64.7 us
    ppermute x2, waiting for transfers between devices, from_partner(): return lax.ppermute(block, axis, route)  45.1 us
    all_gather x1, waiting for transfers between devices, body(): full_rows = lax.all_gather(inputs, 'tensor', axis=1, tiled=True)  43.4 us
    all_gather x1, blocking collectives, body(): lax.all_gather(docs_pair, 'ctx', axis=1, tiled=True)  16.7 us
    all_gather x1, waiting for transfers between devices, body(): lax.all_gather(value_projection_weight[0], 'ctx', axis=0, tiled=True)  15.5 us
    all_gather x1, blocking collectives, body(): lax.all_gather(value_rows.reshape(2, tok_rows, key_width), 'ctx', axis=1,...  12.5 us
  transfers between devices with their start and end apart: 8, of which 7 were waited for; matrix products, arithmetic and copies ran while one was open for 8% of the time, Pallas kernels for 0%

profile of v1, /device:TPU:1, one launch (start us, length us, event | category | flops | bytes accessed | tf_op | source)
XLA Modules:
  0.0 464.1 jit_solution(10069271927594653530)
XLA Ops:
  7.2 0.0 copy-start.1
  7.2 0.0 all-gather.8.cloned.1.call-start
  7.2 3.9 collective-permute-start
  11.1 22.4 %collective-permute-done = bf16[1,256,1024]{2,1,0:T(8,128)(2,1)S(1)} collective-permute-done((bf16[1,256,1024]{2,1,0:T(8,128)(2,1)}, bf16[1,256,1024]{2,1,0:T(8,128)(2,1)S(1)}, u32[]{:S(2)}, u32[]{:S(2)}) %collective-permute-start) | collective-permute-done | bytes 524320 | tf_op jit(solution)/shard_map/ppermute | solution.py:21
  33.6 2.1 pad_maximum_fusion
  35.7 0.0 all-gather.8.cloned.1.call-update
  35.7 0.0 all-gather.10.cloned.1.call-start
  35.7 0.7 all-gather.10.cloned.1.call-update
  36.5 0.0 all-gather.12.cloned.1.call-start
  36.5 0.7 all-gather.12.cloned.1.call-update
  37.2 0.0 all-gather.14.cloned.1.call-start
  37.2 0.5 all-gather.14.cloned.1.call-update
  37.8 2.1 stack.7
  39.9 4.7 %all-to-all-start = ((bf16[4,1024,128]{2,1,0:T(8,128)(2,1)}), bf16[4,1024,128]{2,1,0:T(8,128)(2,1)S(1)}, u32[]{:S(2)}, u32[]{:S(2)}) async-start(bf16[4,1024,128]{2,1,0:T(8,128)(2,1)} %stack.7), calls=%async_computation | async-start | bytes 2097152 | tf_op jit(solution)/shard_map/all_to_all | solution.py:100
  44.6 16.7 %all_gather.24 = s32[2,1024]{1,0:T(2,128)S(1)} all-gather(s32[2,256]{1,0:T(2,128)S(1)} %pad_add_fusion), channel_id=1, replica_groups=mesh['section'=16,'ctx'=4,'tensor'=4] {'ctx'}, dimensions={1}, use_global_device_ids=true | all-gather | bytes 10240 | tf_op jit(solution)/shard_map/all_gather | solution.py:118
  61.3 0.7 fusion.35
  62.0 1.0 multiply_cosine_fusion
  63.0 43.4 %all-gather.8.cloned.1.call-done = bf16[512,4096]{1,0:T(8,128)(2,1)} async-done(((bf16[512,1024]{1,0:T(8,128)(2,1)}), bf16[512,4096]{1,0:T(8,128)(2,1)}) %all-gather.8.cloned.1.call-update) | async-done | bytes 4194320 | tf_op jit(solution)/shard_map/all_gather | solution.py:94
  106.4 3.1 fusion
  109.5 0.0 all-to-all-done
  109.5 3.8 convolution_bitcast_fusion
  113.3 0.6 fusion.50
  113.9 0.1 copy.20
  114.0 15.5 %all-gather.10.cloned.1.call-done = bf16[1,4096,128]{2,1,0:T(8,128)(2,1)} async-done(((bf16[1,1024,128]{2,1,0:T(8,128)(2,1)}), bf16[1,4096,128]{2,1,0:T(8,128)(2,1)}) %all-gather.10.cloned.1.call-update) | async-done | bytes 1048592 | tf_op jit(solution)/shard_map/all_gather | solution.py:102
  129.5 3.8 convolution_convert_fusion
  133.3 0.1 copy.12
  133.4 11.3 %all_gather.25 = bf16[2,1024,128]{2,1,0:T(8,128)(2,1)S(1)} all-gather(bf16[2,256,128]{2,1,0:T(8,128)(2,1)S(1)} %bitcast.132), channel_id=1, replica_groups=mesh['section'=16,'ctx'=4,'tensor'=4] {'ctx'}, dimensions={1}, use_global_device_ids=true | all-gather | bytes 655360 | tf_op jit(solution)/shard_map/all_gather | solution.py:116
  144.8 12.5 %all_gather.23 = bf16[2,1024,128]{1,2,0:T(8,128)(2,1)S(1)} all-gather(bf16[2,256,128]{1,2,0:T(8,128)(2,1)S(1)} %copy.12), channel_id=1, replica_groups=mesh['section'=16,'ctx'=4,'tensor'=4] {'ctx'}, dimensions={1}, use_global_device_ids=true | all-gather | bytes 655360 | tf_op jit(solution)/shard_map/all_gather | solution.py:117
  157.3 64.7 %all-gather.12.cloned.1.call-done = bf16[1,4096,1024]{2,1,0:T(8,128)(2,1)} async-done(((bf16[1,1024,1024]{2,1,0:T(8,128)(2,1)}), bf16[1,4096,1024]{2,1,0:T(8,128)(2,1)}) %all-gather.12.cloned.1.call-update) | async-done | bytes 8388624 | tf_op jit(solution)/shard_map/all_gather | solution.py:98
  222.0 8.2 %fusion.21 = f32[64,8,8,128]{3,1,2,0:T(8,128)S(1)} fusion(bf16[1,4096,1024]{2,1,0:T(8,128)(2,1)} %all-gather.12.cloned.1.call-done, bf16[512,4096]{1,0:T(8,128)(2,1)} %all-gather.8.cloned.1.call-done, f32[4096]{0:T(1024)S(1)} %bitcast.139, f32[512]{0:T(512)S(1)} %add_rsqrt_fusion), kind=kOutput, calls=%fused_computation.28 | convolution fusion | flops 4303355904 | bytes 14698496 | tf_op jit(solution)/shard_map/dot_general | solution.py:105
  230.3 0.5 copy.23
  230.8 0.7 fusion.63
  231.4 0.8 subtract_convert_fusion
  232.2 1.6 fusion.11
  233.9 1.6 fusion.12
  235.5 3.7 fusion.7
  239.2 2.3 divide_convert_fusion.1
  241.5 2.2 divide_convert_fusion
  243.7 66.3 %all-gather.14.cloned.1.call-done = bf16[1,1024,4096]{2,1,0:T(8,128)(2,1)} async-done(((bf16[1,1024,1024]{2,1,0:T(8,128)(2,1)}), bf16[1,1024,4096]{2,1,0:T(8,128)(2,1)}) %all-gather.14.cloned.1.call-update) | async-done | bytes 8388624 | tf_op jit(solution)/shard_map/all_gather | solution.py:103
  310.0 10.2 %fusion.3 = f32[512,4096]{1,0:T(8,128)} fusion(bf16[1,1024,4096]{2,1,0:T(8,128)(2,1)} %all-gather.14.cloned.1.call-done, bf16[256,1024]{0,1:T(8,128)(2,1)S(1)} %bitcast.131, bf16[256,1024]{0,1:T(8,128)(2,1)S(1)} %bitcast.130), kind=kOutput, calls=%fused_computation.7 | convolution fusion | flops 4297064448 | bytes 17825792 | tf_op jit(solution)/shard_map/dot_general | solution.py:135
  320.2 0.0 reduce-scatter.2.cloned.1.call-update
  320.2 1.0 copy-done
  321.3 2.3 collective-permute-start.1
  323.5 22.7 %collective-permute-done.1 = bf16[1,256,1024]{2,1,0:T(8,128)(2,1)S(1)} collective-permute-done((bf16[1,256,1024]{2,1,0:T(8,128)(2,1)S(1)}, bf16[1,256,1024]{2,1,0:T(8,128)(2,1)S(1)}, u32[]{:S(2)}, u32[]{:S(2)}) %collective-permute-start.1) | collective-permute-done | bytes 524320 | tf_op jit(solution)/shard_map/ppermute | solution.py:21
  346.2 107.6 %reduce-scatter.2.cloned.1.call-done = f32[512,1024]{1,0:T(8,128)} async-done(((f32[512,4096]{1,0:T(8,128)}), f32[512,1024]{1,0:T(8,128)}) %reduce-scatter.2.cloned.1.call-update) | async-done | bytes 2097168 | tf_op jit(solution)/shard_map/reduce_scatter | solution.py:136
  453.8 1.9 add_convert_fusion
  455.8 1.0 slice_bitcast_fusion
  456.8 0.8 copy.29
  (15 shorter events, 0.1 us)
Async XLA Ops:
  7.2 37.4 %copy-start.1 = (bf16[1,4096]{1,0:T(2,128)(2,1)S(1)}, bf16[1,4096]{1,0:T(2,128)(2,1)}, u32[]{:S(2)}) copy-start(bf16[1,4096]{1,0:T(2,128)(2,1)} %param.13) | copy-start | bytes 24580
  7.2 37.4 %copy-start.2 = (s32[1,256]{1,0:T(1,128)S(1)}, s32[1,256]{1,0:T(1,128)}, u32[]{:S(2)}) copy-start(s32[1,256]{1,0:T(1,128)} %param.11) | copy-start | bytes 3076
  7.2 37.4 %copy-start.3 = (s32[1,256]{1,0:T(1,128)S(1)}, s32[1,256]{1,0:T(1,128)}, u32[]{:S(2)}) copy-start(s32[1,256]{1,0:T(1,128)} %param.12) | copy-start | bytes 3076
  7.2 99.2 %all-gather.8.cloned.1.call-start = ((), (), s32[]{:S(2)}) async-start(), calls=%async_computation.2 | async-start | bytes 5242880 | tf_op jit(solution)/shard_map/all_gather | solution.py:94
  7.2 26.3 %collective-permute-start = (bf16[1,256,1024]{2,1,0:T(8,128)(2,1)}, bf16[1,256,1024]{2,1,0:T(8,128)(2,1)S(1)}, u32[]{:S(2)}, u32[]{:S(2)}) collective-permute-start(bf16[1,256,1024]{2,1,0:T(8,128)(2,1)} %param.10), channel_id=1, source_target_pairs={{0,128},{128,0},{16,144},{144,16},{32,160},{160,32},{48,176},{176,... | collective-permute-start | bytes 1572872 | tf_op jit(solution)/shard_map/ppermute | solution.py:21
  35.7 93.8 %all-gather.10.cloned.1.call-start = ((), (), s32[]{:S(2)}) async-start(), calls=%async_computation.4 | async-start | bytes 1310720 | tf_op jit(solution)/shard_map/all_gather | solution.py:102
  36.5 185.6 %all-gather.12.cloned.1.call-start = ((), (), s32[]{:S(2)}) async-start(), calls=%async_computation.5 | async-start | bytes 10485760 | tf_op jit(solution)/shard_map/all_gather | solution.py:98
  37.2 272.8 %all-gather.14.cloned.1.call-start = ((), (), s32[]{:S(2)}) async-start(), calls=%async_computation.6 | async-start | bytes 10485760 | tf_op jit(solution)/shard_map/all_gather | solution.py:103
  39.9 69.6 %all-to-all-start = ((bf16[4,1024,128]{2,1,0:T(8,128)(2,1)}), bf16[4,1024,128]{2,1,0:T(8,128)(2,1)S(1)}, u32[]{:S(2)}, u32[]{:S(2)}) async-start(bf16[4,1024,128]{2,1,0:T(8,128)(2,1)} %stack.7), calls=%async_computation | async-start | bytes 2097152 | tf_op jit(solution)/shard_map/all_to_all | solution.py:100
  44.6 409.3 %reduce-scatter.2.cloned.1.call-start = ((), (), s32[]{:S(2)}) async-start(), calls=%async_computation.3 | async-start | bytes 10485760 | tf_op jit(solution)/shard_map/reduce_scatter | solution.py:136
  320.2 1.0 copy-start
  321.3 25.0 %collective-permute-start.1 = (bf16[1,256,1024]{2,1,0:T(8,128)(2,1)S(1)}, bf16[1,256,1024]{2,1,0:T(8,128)(2,1)S(1)}, u32[]{:S(2)}, u32[]{:S(2)}) collective-permute-start(bf16[1,256,1024]{2,1,0:T(8,128)(2,1)S(1)} %copy-done), channel_id=1, source_target_pairs={{0,128},{128,0},{16,144},{144,16},{32,160},{160,32},{48,176},{176,... | collective-permute-start | bytes 1572872 | tf_op jit(solution)/shard_map/ppermute | solution.py:21
Sparse Core Ops, SparseCore 0:
  35.8 70.5 all-gather.7
  108.2 21.2 all-gather.9
  131.3 90.6 all-gather.11
  223.7 86.2 all-gather.13
  320.4 133.4 reduce-scatter.1
